TPU v7x, 32 devices: a whole 2x2x4 slice. The times are simulated.
32 devices in a mesh: dp: 8 (over z, y), chan: 4 (over x, core).
Axes of the slice: x: 2, y: 2, z: 4, core: 2. Of those that a mesh axis runs over, the one named last changes fastest.
Arguments:
- images: bfloat16 [256, 10, 14, 1536], P('dp', None, None, 'chan'), may hold values from -6 to 6
- aspect: int32 [256], P('dp'), may hold values from 0 to 1
- reduce_weight: bfloat16 [1536, 768], P('chan'), may hold values from -400 to 400
- reduce_gain: float32 [768], replicated, may hold values from 0.1 to 1.9
- reduce_bias: float32 [768], replicated, may hold values from -3 to 3
- first_weight: bfloat16 [3, 3, 128, 768], replicated, may hold values from -6 to 6
- first_gain: float32 [768], replicated, may hold values from 0.1 to 1.9
- first_bias: float32 [768], replicated, may hold values from -3 to 3
- second_weight: bfloat16 [3, 3, 128, 768], replicated, may hold values from -6 to 6
- second_gain: float32 [768], replicated, may hold values from 0.1 to 1.9
- second_bias: float32 [768], replicated, may hold values from -3 to 3
- expand_weight: bfloat16 [768, 1536], P('chan'), may hold values from -400 to 400
- expand_gain: float32 [1536], P('chan'), may hold values from 0.1 to 1.9
- expand_bias: float32 [1536], P('chan'), may hold values from -3 to 3
- excite_down: bfloat16 [1536, 768], P('chan'), may hold values from -0.3125 to 0.3125
- excite_down_bias: float32 [768], replicated, may hold values from -3 to 3
- excite_up: bfloat16 [768, 1536], P(None, 'chan'), may hold values from -0.4375 to 0.4375
- excite_up_bias: float32 [1536], P('chan'), may hold values from -3 to 3
- skip_gain: float32 [1], replicated, may hold values from 3 to 6
- out_grad: bfloat16 [256, 10, 14, 1536], P('dp', None, None, 'chan'), may hold values from -6 to 6
Outputs:
- block_out: bfloat16 [256, 10, 14, 1536], P('dp', None, None, 'chan')
- images_grad: float32 [256, 10, 14, 1536], P('dp', None, None, 'chan')
- reduce_weight_grad: float32 [1536, 768], P('chan')
- reduce_gain_grad: float32 [768], replicated
- reduce_bias_grad: float32 [768], replicated
- first_weight_grad: float32 [3, 3, 128, 768], replicated
- first_gain_grad: float32 [768], replicated
- first_bias_grad: float32 [768], replicated
- second_weight_grad: float32 [3, 3, 128, 768], replicated
- second_gain_grad: float32 [768], replicated
- second_bias_grad: float32 [768], replicated
- expand_weight_grad: float32 [768, 1536], P('chan')
- expand_gain_grad: float32 [1536], P('chan')
- expand_bias_grad: float32 [1536], P('chan')
- excite_down_grad: float32 [1536, 768], P('chan')
- excite_down_bias_grad: float32 [768], replicated
- excite_up_grad: float32 [768, 1536], P(None, 'chan')
- excite_up_bias_grad: float32 [1536], P('chan')
- skip_gain_grad: float32 [1], replicated
Inputs may be any that keep to these rules, and one draw needn't show every extreme that they name: `aspect`: 0: the image is 10 rows by 14 columns as stored; 1: it is 14 rows by 10 columns, stored transposed.
All inputs are finite; a program needn't handle non-finite values.
Results may differ from a plain program's by a relative error of at most 0.025.
The roundings to bfloat16 on the way count: a program that leaves them out, or rounds other values in their place, can miss the bound.
Values may be sent and summed in bfloat16 or wider, within the bound.
A program may use at most 256 MiB of HBM per device.

v0:
```python
import jax
import jax.numpy as jnp
from jax import lax
from jax.sharding import PartitionSpec as P

INV_BETA = 1.0 / 1.16619037896906
ALPHA_RES = 0.2
GELU_SCALE = 1.7015
STD_EPSILON = 0.0001
PRECISE = lax.Precision.HIGHEST
NUMBERS = ("NHWC", "HWIO", "NHWC")


def gelu_scaled(value):
    return GELU_SCALE * jax.nn.gelu(value, approximate=True)


def gelu_plain(value):
    return jax.nn.gelu(value, approximate=True)


def backward_of(function, primal, cotangent):
    _, pullback = jax.vjp(function, primal)
    return pullback(cotangent)[0]


def standardize(weight, axes):
    middle = jnp.mean(weight, axis=axes, keepdims=True)
    centered = weight - middle
    spread = jnp.mean(centered * centered, axis=axes, keepdims=True)
    fan_in = 1
    for dimension in axes:
        fan_in = fan_in * weight.shape[dimension]
    return centered * lax.rsqrt(spread * fan_in + STD_EPSILON)


def standardize_group(weight):
    return standardize(weight, (0, 1, 2))


def column_moments(total, squares, fan_in):
    middle = total / fan_in
    spread = squares / fan_in - middle * middle
    return (middle, lax.rsqrt(spread * fan_in + STD_EPSILON))


def standard_grad(summed, centered, rate, column_sum, column_cross, fan_in):
    return rate * (summed - column_sum / fan_in) - rate * rate * rate * centered * column_cross


def group_conv(values, kernel, groups):
    return lax.conv_general_dilated(
        values,
        kernel,
        (1, 1),
        "SAME",
        dimension_numbers=NUMBERS,
        feature_group_count=groups,
        preferred_element_type=jnp.float32,
    )


def group_input_grad(cotangent, kernel, groups):
    taps = kernel.shape[2]
    parted = kernel.reshape(3, 3, taps, groups, taps)
    swapped = jnp.transpose(parted, (0, 1, 4, 3, 2)).reshape(3, 3, taps, groups * taps)[::-1, ::-1]
    return group_conv(cotangent, swapped, groups)


def group_weight_grad(values, cotangent, groups):
    height, width = (values.shape[1], values.shape[2])
    taps = values.shape[3] // groups
    padded = jnp.pad(values, ((0, 0), (1, 1), (1, 1), (0, 0)))
    parted_grad = cotangent.reshape(cotangent.shape[:3] + (groups, taps))
    kernel_rows = []
    for shift_h in range(3):
        row_terms = []
        for shift_w in range(3):
            window = padded[:, shift_h : shift_h + height, shift_w : shift_w + width, :]
            window = window.reshape(window.shape[:3] + (groups, taps))
            product = jnp.einsum(
                "nhwgi,nhwgo->igo", window, parted_grad, preferred_element_type=jnp.float32
            )
            row_terms.append(product.reshape(taps, groups * taps))
        kernel_rows.append(jnp.stack(row_terms))
    return jnp.stack(kernel_rows)


def oriented_conv(values, kernel, aspects, groups):
    plain = group_conv(values, kernel, groups)
    turned = group_conv(values, jnp.transpose(kernel, (1, 0, 2, 3)), groups)
    return jnp.where((aspects == 1)[:, None, None, None], turned, plain)


def oriented_back(values, cotangent, kernel, aspects, groups):
    turned_mask = (aspects == 1)[:, None, None, None]
    nothing = jnp.zeros_like(cotangent)
    grad_plain = jnp.where(turned_mask, nothing, cotangent)
    grad_turned = jnp.where(turned_mask, cotangent, nothing)
    kernel_turned = jnp.transpose(kernel, (1, 0, 2, 3))
    grad_values = group_input_grad(grad_plain, kernel, groups) + group_input_grad(
        grad_turned, kernel_turned, groups
    )
    grad_kernel = group_weight_grad(values, grad_plain, groups)
    grad_kernel = grad_kernel + jnp.transpose(
        group_weight_grad(values, grad_turned, groups), (1, 0, 2, 3)
    )
    return (grad_values, grad_kernel)


def body(
    images,
    aspect,
    reduce_weight,
    reduce_gain,
    reduce_bias,
    first_weight,
    first_gain,
    first_bias,
    second_weight,
    second_gain,
    second_bias,
    expand_weight,
    expand_gain,
    expand_bias,
    excite_down,
    excite_down_bias,
    excite_up,
    excite_up_bias,
    skip_gain,
    out_grad,
):
    parts = lax.axis_size("chan")
    index = lax.axis_index("chan")
    n_images = images.shape[0]
    share = n_images // parts
    groups = first_weight.shape[3] // first_weight.shape[2]
    mid_share = expand_weight.shape[0]
    in_share = reduce_weight.shape[0]
    pixel_count = images.shape[1] * images.shape[2]
    reduce_fan = in_share * parts
    expand_fan = mid_share * parts
    reduce32 = reduce_weight.astype(jnp.float32)
    expand32 = expand_weight.astype(jnp.float32)
    moments = lax.psum(
        (
            jnp.sum(reduce32, axis=0),
            jnp.sum(reduce32 * reduce32, axis=0),
            jnp.sum(expand32, axis=0),
            jnp.sum(expand32 * expand32, axis=0),
        ),
        "chan",
    )
    reduce_mean, reduce_rate = column_moments(moments[0], moments[1], reduce_fan)
    expand_mean, expand_rate = column_moments(moments[2], moments[3], expand_fan)
    reduce_center = reduce32 - reduce_mean
    expand_center = expand32 - expand_mean
    kernel_reduce = (reduce_center * reduce_rate).astype(jnp.bfloat16)
    kernel_expand = (expand_center * expand_rate).astype(jnp.bfloat16)
    kernel_first = standardize_group(first_weight.astype(jnp.float32)).astype(jnp.bfloat16)
    kernel_second = standardize_group(second_weight.astype(jnp.float32)).astype(jnp.bfloat16)
    scaled = (images.astype(jnp.float32) * INV_BETA).astype(jnp.bfloat16)
    aspects = lax.dynamic_slice_in_dim(aspect, index * share, share, 0)
    rows = scaled
    pre_reduce = lax.psum_scatter(
        jnp.einsum("nhwc,cm->nhwm", rows, kernel_reduce, preferred_element_type=jnp.float32),
        "chan",
        scatter_dimension=0,
        tiled=True,
    )
    out_reduce = reduce_gain * pre_reduce + reduce_bias
    act_reduce = gelu_scaled(out_reduce).astype(jnp.bfloat16)
    pre_first = oriented_conv(act_reduce, kernel_first, aspects, groups)
    out_first = first_gain * pre_first + first_bias
    act_first = gelu_scaled(out_first).astype(jnp.bfloat16)
    pre_second = oriented_conv(act_first, kernel_second, aspects, groups)
    out_second = second_gain * pre_second + second_bias
    act_second = gelu_scaled(out_second).astype(jnp.bfloat16)
    act_columns = lax.all_to_all(act_second, "chan", split_axis=3, concat_axis=0, tiled=True)
    partials = jnp.einsum(
        "nhwm,mc->nhwc", act_columns, kernel_expand, preferred_element_type=jnp.float32
    )
    pre_expand = lax.psum_scatter(
        partials.astype(jnp.bfloat16), "chan", scatter_dimension=3, tiled=True
    ).astype(jnp.float32)
    out_expand = expand_gain * pre_expand + expand_bias
    pooled = jnp.mean(out_expand, axis=(1, 2))
    down_partial = jnp.dot(pooled, excite_down.astype(jnp.float32), precision=PRECISE)
    down = lax.psum(down_partial, "chan") + excite_down_bias
    hidden = gelu_plain(down)
    upper = jnp.dot(hidden, excite_up.astype(jnp.float32), precision=PRECISE) + excite_up_bias
    sigma = jax.nn.sigmoid(upper)
    gating = 2.0 * sigma
    branch = out_expand * gating[:, None, None, :]
    branch_scale = ALPHA_RES * skip_gain[0]
    block_out = (images.astype(jnp.float32) + branch_scale * branch).astype(jnp.bfloat16)
    grad_out = out_grad.astype(jnp.float32)
    skip_term = ALPHA_RES * jnp.sum(grad_out * branch)
    grad_branch = branch_scale * grad_out
    grad_gating = jnp.sum(grad_branch * out_expand, axis=(1, 2))
    grad_upper = grad_gating * 2.0 * sigma * (1.0 - sigma)
    excite_up_bias_grad = jnp.sum(grad_upper, axis=0)
    excite_up_grad = jnp.dot(hidden.T, grad_upper, precision=PRECISE)
    hidden_partial = jnp.dot(grad_upper, excite_up.astype(jnp.float32).T, precision=PRECISE)
    grad_hidden = lax.psum(hidden_partial.astype(jnp.bfloat16), "chan").astype(jnp.float32)
    grad_down = backward_of(gelu_plain, down, grad_hidden)
    excite_down_bias_grad = jnp.sum(grad_down, axis=0)
    excite_down_grad = jnp.dot(pooled.T, grad_down, precision=PRECISE)
    grad_pooled = jnp.dot(grad_down, excite_down.astype(jnp.float32).T, precision=PRECISE)
    grad_expand = (
        grad_branch * gating[:, None, None, :] + grad_pooled[:, None, None, :] / pixel_count
    )
    expand_gain_grad = jnp.sum(grad_expand * pre_expand, axis=(0, 1, 2))
    expand_bias_grad = jnp.sum(grad_expand, axis=(0, 1, 2))
    grad_pre_expand = (grad_expand * expand_gain).astype(jnp.bfloat16)
    start_columns = jnp.zeros(act_columns.shape, jnp.float32)
    start_kernel = jnp.zeros((mid_share, expand_weight.shape[1]), jnp.float32)
    piece = lax.all_gather(grad_pre_expand, "chan", axis=3, tiled=True)
    start = jnp.int32(0)
    grad_columns = start_columns
    grad_kernel = start_kernel
    kernel_part = lax.dynamic_slice_in_dim(kernel_expand, start, piece.shape[3], 1)
    grad_columns = grad_columns + jnp.einsum(
        "nhwc,mc->nhwm", piece, kernel_part, preferred_element_type=jnp.float32
    )
    grad_block = jnp.einsum("nhwm,nhwc->mc", act_columns, piece, preferred_element_type=jnp.float32)
    grad_kernel = lax.dynamic_update_slice_in_dim(grad_kernel, grad_block, start, 1)
    grad_columns, expand_rows = (grad_columns, grad_kernel)
    grad_act_second = lax.all_to_all(
        grad_columns.astype(jnp.bfloat16), "chan", split_axis=0, concat_axis=3, tiled=True
    )
    expand_column_sum = jnp.sum(expand_rows, axis=0)
    expand_cross = jnp.sum(expand_rows * expand_center, axis=0)
    expand_full = jnp.zeros((1, 1), jnp.float32)
    grad_second = backward_of(gelu_scaled, out_second, grad_act_second.astype(jnp.float32))
    second_gain_term = jnp.sum(grad_second * pre_second, axis=(0, 1, 2))
    second_bias_term = jnp.sum(grad_second, axis=(0, 1, 2))
    grad_pre_second = (grad_second * second_gain).astype(jnp.bfloat16)
    grad_act_first, grad_kernel_second = oriented_back(
        act_first, grad_pre_second, kernel_second, aspects, groups
    )
    grad_first = backward_of(gelu_scaled, out_first, grad_act_first)
    first_gain_term = jnp.sum(grad_first * pre_first, axis=(0, 1, 2))
    first_bias_term = jnp.sum(grad_first, axis=(0, 1, 2))
    grad_pre_first = (grad_first * first_gain).astype(jnp.bfloat16)
    grad_act_reduce, grad_kernel_first = oriented_back(
        act_reduce, grad_pre_first, kernel_first, aspects, groups
    )
    grad_reduce = backward_of(gelu_scaled, out_reduce, grad_act_reduce)
    reduce_gain_term = jnp.sum(grad_reduce * pre_reduce, axis=(0, 1, 2))
    reduce_bias_term = jnp.sum(grad_reduce, axis=(0, 1, 2))
    grad_pre_reduce = (grad_reduce * reduce_gain).astype(jnp.bfloat16)
    piece = lax.all_gather(grad_pre_reduce, "chan", axis=0, tiled=True)
    rows = scaled
    grad_kernel = jnp.einsum("nhwc,nhwm->cm", rows, piece, preferred_element_type=jnp.float32)
    grad_rows = jnp.einsum(
        "nhwm,cm->nhwc", piece, kernel_reduce, preferred_element_type=jnp.float32
    )
    grad_scaled = grad_rows
    grad_kernel_reduce, grad_scaled = (grad_kernel, grad_scaled)
    images_grad = grad_out + INV_BETA * grad_scaled
    reduce_column_sum = jnp.sum(grad_kernel_reduce, axis=0)
    reduce_cross = jnp.sum(grad_kernel_reduce * reduce_center, axis=0)
    sharded = lax.psum(
        (
            grad_kernel_reduce,
            expand_rows,
            excite_down_grad,
            excite_down_bias_grad,
            excite_up_grad,
            excite_up_bias_grad,
            expand_gain_grad,
            expand_bias_grad,
        ),
        "dp",
    )
    shared = lax.psum(
        (
            grad_kernel_first,
            grad_kernel_second,
            reduce_gain_term,
            reduce_bias_term,
            first_gain_term,
            first_bias_term,
            second_gain_term,
            second_bias_term,
            skip_term,
            reduce_column_sum,
            reduce_cross,
            expand_column_sum,
            expand_cross,
            expand_full,
        ),
        ("dp", "chan"),
    )
    expand_summed = sharded[1]
    reduce_weight_grad = standard_grad(
        sharded[0], reduce_center, reduce_rate, shared[9], shared[10], reduce_fan
    )
    expand_weight_grad = standard_grad(
        expand_summed, expand_center, expand_rate, shared[11], shared[12], expand_fan
    )
    first_weight_grad = backward_of(standardize_group, first_weight.astype(jnp.float32), shared[0])
    second_weight_grad = backward_of(
        standardize_group, second_weight.astype(jnp.float32), shared[1]
    )
    return (
        block_out,
        images_grad,
        reduce_weight_grad,
        shared[2],
        shared[3],
        first_weight_grad,
        shared[4],
        shared[5],
        second_weight_grad,
        shared[6],
        shared[7],
        expand_weight_grad,
        sharded[6],
        sharded[7],
        sharded[2],
        sharded[3],
        sharded[4],
        sharded[5],
        shared[8].reshape(1),
    )


def solution(mesh):
    placed = (
        P("dp", None, None, "chan"),
        P("dp"),
        P("chan", None),
        P(),
        P(),
        P(),
        P(),
        P(),
        P(),
        P(),
        P(),
        P("chan", None),
        P("chan"),
        P("chan"),
        P("chan", None),
        P(),
        P(None, "chan"),
        P("chan"),
        P(),
        P("dp", None, None, "chan"),
    )
    return jax.shard_map(
        body,
        mesh=mesh,
        in_specs=placed,
        out_specs=(
            P("dp", None, None, "chan"),
            P("dp", None, None, "chan"),
            P("chan", None),
            P(),
            P(),
            P(),
            P(),
            P(),
            P(),
            P(),
            P(),
            P("chan", None),
            P("chan"),
            P("chan"),
            P("chan", None),
            P(),
            P(None, "chan"),
            P("chan"),
            P(),
        ),
        check_vma=False,
    )
```

profile of v0, /device:TPU:0, one launch (start us, length us, event | category | flops | bytes accessed | tf_op | source)
XLA Modules:
  0.0 1309.5 jit_solution(16552987430906464153)
XLA Ops:
  9.8 12.8 all-reduce.6
  23.8 10.8 fusion.82
  50.0 92.0 %reduce-scatter.5.cloned.1.call-done = f32[8,10,14,768]{3,0,2,1:T(8,128)} async-done(((f32[32,10,14,768]{3,0,2,1:T(8,128)}), f32[8,10,14,768]{3,0,2,1:T(8,128)}) %reduce-scatter.5.cloned.1.call-update) | async-done | bytes 3440656 | tf_op jit(solution)/shard_map/reduce_scatter | solution.py:165
  169.4 12.9 copy.282
  182.3 37.4 %reshape.338 = bf16[4,2,107520]{2,1,0:T(2,128)(2,1)} reshape(bf16[768,10,8,14]{3,2,1,0:T(8,128)(2,1)} %bitcast.508) | data formatting | bytes 3440640
  224.8 21.1 %all-to-all-done = bf16[4,2,107520]{2,1,0:T(2,128)(2,1)} async-done(((bf16[4,2,107520]{2,1,0:T(2,128)(2,1)}), bf16[4,2,107520]{2,1,0:T(2,128)(2,1)}, u32[]{:S(2)}, u32[]{:S(2)}) %all-to-all-start) | async-done | bytes 1720352 | tf_op jit(solution)/shard_map/all_to_all | solution.py:179
  245.8 42.6 %reshape.339 = bf16[768,10,8,14]{3,2,1,0:T(8,128)(2,1)} reshape(bf16[4,2,107520]{2,1,0:T(2,128)(2,1)} %all-to-all-done) | data formatting | bytes 3440640
  288.4 20.3 %copy.283 = bf16[8,10,14,4,192]{4,0,3,2,1:T(8,128)(2,1)} copy(bf16[8,10,14,4,192]{2,0,1,4,3:T(8,128)(2,1)} %bitcast.510) | data formatting | bytes 3440640 | tf_op jit(solution)/shard_map/all_to_all | solution.py:179
  317.3 83.1 %copy.341 = bf16[32,10,14,1536]{0,2,1,3:T(8,128)(2,1)} copy(bf16[32,10,14,1536]{3,0,2,1:T(8,128)(2,1)} %convolution_convert_fusion) | data formatting | bytes 27525120
  400.4 72.3 %reshape.336 = bf16[1536,4480]{1,0:T(8,128)(2,1)} reshape(bf16[1536,10,14,32]{3,2,1,0:T(8,128)(2,1)} %bitcast.507) | data formatting | bytes 27525120
  473.4 106.3 %reduce-scatter.7.cloned.1.call-done = bf16[384,4480]{1,0:T(8,128)(2,1)} async-done(((bf16[1536,4480]{1,0:T(8,128)(2,1)}), bf16[384,4480]{1,0:T(8,128)(2,1)}) %reduce-scatter.7.cloned.1.call-update) | async-done | bytes 3440656
  579.7 18.3 %reshape.337 = bf16[384,10,14,32]{3,2,1,0:T(8,128)(2,1)} reshape(bf16[384,4480]{1,0:T(8,128)(2,1)} %reduce-scatter.7.cloned.1.call-done) | data formatting | bytes 6881280
  598.0 18.6 %copy.342 = bf16[32,10,14,384]{3,0,2,1:T(8,128)(2,1)} copy(bf16[32,10,14,384]{0,2,1,3:T(8,128)(2,1)} %bitcast.509) | data formatting | bytes 6881280
  622.6 31.4 %all-reduce.11.cloned.1.call-done = f32[32,768]{1,0:T(8,128)} async-done(((f32[32,768]{1,0:T(8,128)}), f32[32,768]{1,0:T(8,128)}) %all-reduce.11.cloned.1.call-update) | async-done | bytes 98320 | tf_op jit(solution)/shard_map/psum | solution.py:189
  655.9 10.6 psum.194
  722.6 37.5 %all-reduce.4 = (f32[384]{0:T(512)}, f32[384]{0:T(512)}, f32[768]{0:T(1024)}, f32[384]{0:T(512)}) all-reduce(f32[384]{0:T(512)S(1)} %get-tuple-element.96, f32[384]{0:T(512)S(1)} %get-tuple-element.99, f32[768]{0:T(1024)S(1)} %get-tuple-element.139, f32[384]{0:T(512)S(1)} %get-tuple-element.148), channel_id=1, replica_groups=mesh['dp'=8,'chan'=4] {'dp'}, use_global_device_ids=true, to_apply=%region_47.48 | all-reduce | flops 1920 | bytes 15360 | tf_op jit(solution)/shard_map/psum | solution.py:264
  783.6 9.5 fusion.272
  793.1 21.6 %all-to-all-done.1 = bf16[32,10,14,192]{3,2,1,0:T(8,128)(2,1)} async-done(((bf16[32,10,14,192]{3,2,1,0:T(8,128)(2,1)}), bf16[32,10,14,192]{3,2,1,0:T(8,128)(2,1)}, u32[]{:S(2)}, u32[]{:S(2)}) %all-to-all-start.1) | async-done | bytes 1720352 | tf_op jit(solution)/shard_map/all_to_all | solution.py:229
  918.0 9.6 fusion.269
  927.8 18.1 %all-gather.5.cloned.1.call-done = bf16[32,10,14,768]{3,0,2,1:T(8,128)(2,1)} async-done(((bf16[8,10,14,768]{3,0,2,1:T(8,128)(2,1)}), bf16[32,10,14,768]{3,0,2,1:T(8,128)(2,1)}) %all-gather.5.cloned.1.call-update) | async-done | bytes 6881296 | tf_op jit(solution)/shard_map/all_gather | solution.py:253
  957.4 160.8 %all-reduce.13.cloned.1.call-done = (f32[3,3,128,768]{2,3,0,1:T(8,128)}, f32[3,3,128,768]{2,3,0,1:T(8,128)}) async-done(((f32[3,3,128,768]{2,3,0,1:T(8,128)}, f32[3,3,128,768]{2,3,0,1:T(8,128)}), (f32[3,3,128,768]{2,3,0,1:T(8,128)}, f32[3,3,128,768]{2,3,0,1:T(8,128)})) %all-reduce.13.cloned.1.call-update) | async-done | bytes 7077904 | tf_op jit(solution)/shard_map/psum | solution.py:277
  1144.3 47.2 %all-reduce.2 = (f32[768]{0:T(1024)S(1)}, f32[768]{0:T(1024)S(1)}, f32[768]{0:T(1024)}, f32[768]{0:T(1024)}, f32[768]{0:T(1024)}, /*index=5*/f32[768]{0:T(1024)}...) all-reduce(f32[768]{0:T(1024)S(1)} %get-tuple-element.109, ...), channel_id=1, replica_groups=mesh['dp'=8,'chan'=4] {'dp','chan'}, use_global_device_ids=true, to_apply=%region_22.23 | all-reduce | flops 9217 | bytes 73736 | tf_op jit(solution)/shard_map/psum | solution.py:277
  1191.6 10.7 convert_add_fusion
  1202.2 93.5 %all-reduce.15.cloned.1.call-done = (f32[384,768]{1,0:T(8,128)}, f32[192,1536]{1,0:T(8,128)}, f32[384,768]{1,0:T(8,128)}, f32[768,384]{1,0:T(8,128)}) async-done(((f32[384,768]{1,0:T(8,128)}, f32[192,1536]{1,0:T(8,128)}, f32[384,768]{1,0:T(8,128)}, f32[768,384]{1,0:T(8,128)}), (f32[384,768]{1,0:T(8,128)}, f32[192,1536]{1,0:T(8,128)}, f32[384,768]{1,0:T(8,128)}, ...) | async-done | bytes 4718608 | tf_op jit(solution)/shard_map/psum | solution.py:264
  (350 shorter events, 294.0 us)
Async XLA Ops:
  7.2 646.8 %copy-start = (bf16[768,384]{1,0:T(8,128)(2,1)S(1)}, bf16[768,384]{1,0:T(8,128)(2,1)}, u32[]{:S(2)}) copy-start(bf16[768,384]{1,0:T(8,128)(2,1)} %param.36) | copy-start | bytes 1769476
  7.2 134.7 %reduce-scatter.5.cloned.1.call-start = ((), (), s32[]{:S(2)}) async-start(), calls=%async_computation.4 | async-start | bytes 17203200 | tf_op jit(solution)/shard_map/reduce_scatter | solution.py:165
  48.6 93.4 %copy-start.87 = (f32[768]{0:T(1024)S(1)}, f32[768]{0:T(1024)}, u32[]{:S(2)}) copy-start(f32[768]{0:T(1024)} %param.24) | copy-start | bytes 9220
  48.6 93.4 %copy-start.89 = (f32[768]{0:T(1024)S(1)}, f32[768]{0:T(1024)}, u32[]{:S(2)}) copy-start(f32[768]{0:T(1024)} %param.23) | copy-start | bytes 9220
  50.0 815.1 %copy-start.91 = (pred[8]{0:T(512)(128)(4,1)}, pred[8]{0:T(512)(128)(4,1)S(1)}, u32[]{:S(2)}) copy-start(pred[8]{0:T(512)(128)(4,1)S(1)} %dynamic-slice_compare_fusion) | copy-start | bytes 28
  50.0 95.4 %copy-start.25 = (bf16[3,3,128,768]{2,3,1,0:T(8,128)(2,1)S(1)}, bf16[3,3,128,768]{2,3,1,0:T(8,128)(2,1)}, u32[]{:S(2)}) copy-start(bf16[3,3,128,768]{2,3,1,0:T(8,128)(2,1)} %copy.279) | copy-start | bytes 5308420
  219.7 26.1 %all-to-all-start = ((bf16[4,2,107520]{2,1,0:T(2,128)(2,1)}), bf16[4,2,107520]{2,1,0:T(2,128)(2,1)}, u32[]{:S(2)}, u32[]{:S(2)}) async-start(bf16[4,2,107520]{2,1,0:T(2,128)(2,1)} %reshape.338), calls=%async_computation.1 | async-start | bytes 3440640 | tf_op jit(solution)/shard_map/all_to_all | solution.py:179
  224.1 355.6 %reduce-scatter.7.cloned.1.call-start = ((), (), s32[]{:S(2)}) async-start(), calls=%async_computation.8 | async-start | bytes 17203200
  224.8 542.3 %copy-start.62 = (f32[1536]{0:T(1024)}, f32[1536]{0:T(1024)S(1)}, u32[]{:S(2)}) copy-start(f32[1536]{0:T(1024)S(1)} %get-tuple-element.151) | copy-start | bytes 18436
  224.8 558.8 %copy-start.60 = (f32[1536]{0:T(1024)}, f32[1536]{0:T(1024)S(1)}, u32[]{:S(2)}) copy-start(f32[1536]{0:T(1024)S(1)} %get-tuple-element.152) | copy-start | bytes 18436
  472.7 181.3 %all-reduce.11.cloned.1.call-start = ((), (), s32[]{:S(2)}) async-start(), calls=%async_computation.5 | async-start | bytes 196608 | tf_op jit(solution)/shard_map/psum | solution.py:189
  622.5 144.6 %all-gather.3.cloned.1.call-start = ((), (), s32[]{:S(2)}) async-start(), calls=%async_computation.6 | async-start | bytes 17203200 | tf_op jit(solution)/shard_map/all_gather | solution.py:218
  778.6 36.1 %all-to-all-start.1 = ((bf16[32,10,14,192]{3,2,1,0:T(8,128)(2,1)}), bf16[32,10,14,192]{3,2,1,0:T(8,128)(2,1)}, u32[]{:S(2)}, u32[]{:S(2)}) async-start(bf16[32,10,14,192]{3,2,1,0:T(8,128)(2,1)} %copy.284), calls=%async_computation.2 | async-start | bytes 5242880 | tf_op jit(solution)/shard_map/all_to_all | solution.py:229
  783.3 162.6 %all-gather.5.cloned.1.call-start = ((), (), s32[]{:S(2)}) async-start(), calls=%async_computation.7 | async-start | bytes 8601600 | tf_op jit(solution)/shard_map/all_gather | solution.py:253
  896.0 222.2 %all-reduce.13.cloned.1.call-start = ((), (), s32[]{:S(2)}) async-start(), calls=%async_computation.9 | async-start | bytes 14155776 | tf_op jit(solution)/shard_map/psum | solution.py:277
  917.3 378.4 %all-reduce.15.cloned.1.call-start = ((), (), s32[]{:S(2)}) async-start(), calls=%async_computation.10 | async-start | bytes 9437184 | tf_op jit(solution)/shard_map/psum | solution.py:264
  953.9 164.3 %copy-start.59 = (f32[768]{0:T(1024)S(1)}, f32[768]{0:T(1024)}, u32[]{:S(2)}) copy-start(f32[768]{0:T(1024)} %copy-done.58) | copy-start | bytes 9220
  954.0 167.6 %copy-start.75 = (f32[768]{0:T(1024)S(1)}, f32[768]{0:T(1024)}, u32[]{:S(2)}) copy-start(f32[768]{0:T(1024)} %copy-done.74) | copy-start | bytes 9220
  1139.1 52.4 %copy-start.69 = (f32[768]{0:T(1024)S(1)}, f32[768]{0:T(1024)}, u32[]{:S(2)}) copy-start(f32[768]{0:T(1024)} %copy-done.68) | copy-start | bytes 9220
  1191.5 104.2 %copy-start.23 = (bf16[192,1536]{1,0:T(8,128)(2,1)S(1)}, bf16[192,1536]{1,0:T(8,128)(2,1)}, u32[]{:S(2)}) copy-start(bf16[192,1536]{1,0:T(8,128)(2,1)} %param.31) | copy-start | bytes 1769476
  1191.5 104.2 %copy-start.61 = (f32[1536]{0:T(1024)S(1)}, f32[1536]{0:T(1024)}, u32[]{:S(2)}) copy-start(f32[1536]{0:T(1024)} %copy-done.60) | copy-start | bytes 18436
  1191.5 104.2 %copy-start.63 = (f32[1536]{0:T(1024)S(1)}, f32[1536]{0:T(1024)}, u32[]{:S(2)}) copy-start(f32[1536]{0:T(1024)} %copy-done.62) | copy-start | bytes 18436
  1191.5 104.2 %copy-start.76 = (f32[1536]{0:T(1024)S(1)}, f32[1536]{0:T(1024)}, u32[]{:S(2)}) copy-start(f32[1536]{0:T(1024)} %get-tuple-element.150) | copy-start | bytes 18436
  1202.2 96.2 %copy-start.80 = (f32[768]{0:T(1024)S(1)}, f32[768]{0:T(1024)}, u32[]{:S(2)}) copy-start(f32[768]{0:T(1024)} %get-tuple-element.153) | copy-start | bytes 9220
  (87 other events, 471.4 us)
Sparse Core Ops, SparseCore 0:
  34.7 107.1 reduce-scatter.4
  472.8 106.8 reduce-scatter.6
  622.7 31.2 all-reduce.10
  678.3 88.6 all-gather.2
  896.1 49.7 all-gather.4
  953.9 164.2 all-reduce.12
  1123.9 171.7 all-reduce.14
where the time goes:
time: 1320 us; the launch traced here: 1310 us
  waiting for transfers between devices  548 us (42%)
  local copies, waits for them, and re-layouts  398 us (30%)
  matrix products  157 us (12%)
  blocking collectives  108 us (8%)
  other arithmetic  71.2 us (5%)
  between operations  16.8 us (1%)
    unnamed x216, local copies, waits for them, and re-layouts  305 us
    psum x1, waiting for transfers between devices, body(): lax.psum((grad_kernel_first, grad_kernel_second, reduce_gain_term, reduce...  161 us
    unnamed x8, waiting for transfers between devices  106 us
    psum x1, waiting for transfers between devices, body(): lax.psum((grad_kernel_reduce, expand_rows, excite_down_grad, excite_down_...  93.5 us
    reduce_scatter x1, waiting for transfers between devices, body(): lax.psum_scatter(jnp.einsum('nhwc,cm->nhwm', rows, kernel_reduce, preferr...  92 us
    conv_general_dilated x8, matrix products, group_conv(): lax.conv_general_dilated(values, kernel, (1, 1), 'SAME', dimension_number...  47.9 us
    psum x1, blocking collectives, body(): lax.psum((grad_kernel_first, grad_kernel_second, reduce_gain_term, reduce...  47.2 us
    dot_general x36, matrix products, group_weight_grad(): jnp.einsum('nhwgi,nhwgo->igo', window, parted_grad, preferred_element_typ...  44.3 us
  transfers between devices with their start and end apart: 9, of which 9 were waited for; matrix products, arithmetic and copies ran while one was open for 11% of the time, Pallas kernels for 0%

commit v1 on v0

--- a/solution.py
+++ b/solution.py
@@ -275,23 +275,26 @@
         "dp",
     )
     shared = lax.psum(
-        (
-            grad_kernel_first,
-            grad_kernel_second,
-            reduce_gain_term,
-            reduce_bias_term,
-            first_gain_term,
-            first_bias_term,
-            second_gain_term,
-            second_bias_term,
-            skip_term,
-            reduce_column_sum,
-            reduce_cross,
-            expand_column_sum,
-            expand_cross,
-            expand_full,
+        lax.psum(
+            (
+                grad_kernel_first,
+                grad_kernel_second,
+                reduce_gain_term,
+                reduce_bias_term,
+                first_gain_term,
+                first_bias_term,
+                second_gain_term,
+                second_bias_term,
+                skip_term,
+                reduce_column_sum,
+                reduce_cross,
+                expand_column_sum,
+                expand_cross,
+                expand_full,
+            ),
+            "chan",
         ),
-        ("dp", "chan"),
+        "dp",
     )
     expand_summed = sharded[1]
     reduce_weight_grad = standard_grad(

time: 1320 us -> 1510 us (1.14)
  waiting for transfers between devices: 548 us -> 765 us
  blocking collectives: 108 us -> 78.5 us
    psum x1, waiting for transfers between devices: 93.5 us -> 273 us  [body(): lax.psum((grad_kernel_reduce, expand_rows, excite_down_grad, excite_down_...]
    all_gather x1, waiting for transfers between devices: 2.63 us -> 88.9 us  [body(): piece = lax.all_gather(grad_pre_expand, 'chan', axis=3, tiled=True)]
    psum x1, blocking collectives: 47.2 us -> 12.1 us  [body(): lax.psum((grad_kernel_first, grad_kernel_second, reduce_gain_term, reduce...]
    psum x1, waiting for transfers between devices: 161 us -> 128 us  [body(): lax.psum((grad_kernel_first, grad_kernel_second, reduce_gain_term, reduce...]
    all_to_all x1, waiting for transfers between devices: 21.6 us -> 6.25 us  [body(): lax.all_to_all(grad_columns.astype(jnp.bfloat16), 'chan', split_axis=0, c...]
    unnamed x216 -> x232, local copies, waits for them, and re-layouts: 305 us -> 308 us
  transfers between devices with their start and end apart: 9 -> 9, of which waited for: 9 -> 9; matrix products, arithmetic and copies ran while one was open for 11% -> 8% of each run, Pallas kernels for 0% -> 0%
where the time goes in v1:
time: 1510 us; the launch traced here: 1500 us
  waiting for transfers between devices  765 us (51%)
  local copies, waits for them, and re-layouts  400 us (26%)
  matrix products  158 us (10%)
  blocking collectives  78.5 us (5%)
  other arithmetic  71.1 us (5%)
  between operations  17.1 us (1%)
    unnamed x232, local copies, waits for them, and re-layouts  308 us
    psum x1, waiting for transfers between devices, body(): lax.psum((grad_kernel_reduce, expand_rows, excite_down_grad, excite_down_...  273 us
    psum x1, waiting for transfers between devices, body(): lax.psum((grad_kernel_first, grad_kernel_second, reduce_gain_term, reduce...  128 us
    unnamed x8, waiting for transfers between devices  106 us
    reduce_scatter x1, waiting for transfers between devices, body(): lax.psum_scatter(jnp.einsum('nhwc,cm->nhwm', rows, kernel_reduce, preferr...  92 us
    all_gather x1, waiting for transfers between devices, body(): piece = lax.all_gather(grad_pre_expand, 'chan', axis=3, tiled=True)  88.9 us
    conv_general_dilated x8, matrix products, group_conv(): lax.conv_general_dilated(values, kernel, (1, 1), 'SAME', dimension_number...  47.6 us
    dot_general x36, matrix products, group_weight_grad(): jnp.einsum('nhwgi,nhwgo->igo', window, parted_grad, preferred_element_typ...  44.4 us
  transfers between devices with their start and end apart: 9, of which 9 were waited for; matrix products, arithmetic and copies ran while one was open for 8% of the time, Pallas kernels for 0%

profile of v1, /device:TPU:0, one launch (start us, length us, event | category | flops | bytes accessed | tf_op | source)
XLA Modules:
  0.0 1499.7 jit_solution(11915344168946995817)
XLA Ops:
  9.8 12.8 all-reduce.5
  23.8 10.8 fusion.82
  49.9 92.0 %reduce-scatter.5.cloned.1.call-done = f32[8,10,14,768]{3,0,2,1:T(8,128)} async-done(((f32[32,10,14,768]{3,0,2,1:T(8,128)}), f32[8,10,14,768]{3,0,2,1:T(8,128)}) %reduce-scatter.5.cloned.1.call-update) | async-done | bytes 3440656 | tf_op jit(solution)/shard_map/reduce_scatter | solution.py:165
  169.2 12.9 copy.282
  182.1 37.7 %reshape.338 = bf16[4,2,107520]{2,1,0:T(2,128)(2,1)} reshape(bf16[768,10,8,14]{3,2,1,0:T(8,128)(2,1)} %bitcast.508) | data formatting | bytes 3440640
  224.8 21.1 %all-to-all-done = bf16[4,2,107520]{2,1,0:T(2,128)(2,1)} async-done(((bf16[4,2,107520]{2,1,0:T(2,128)(2,1)}), bf16[4,2,107520]{2,1,0:T(2,128)(2,1)}, u32[]{:S(2)}, u32[]{:S(2)}) %all-to-all-start) | async-done | bytes 1720352 | tf_op jit(solution)/shard_map/all_to_all | solution.py:179
  245.9 42.5 %reshape.339 = bf16[768,10,8,14]{3,2,1,0:T(8,128)(2,1)} reshape(bf16[4,2,107520]{2,1,0:T(2,128)(2,1)} %all-to-all-done) | data formatting | bytes 3440640
  288.4 20.3 %copy.283 = bf16[8,10,14,4,192]{4,0,3,2,1:T(8,128)(2,1)} copy(bf16[8,10,14,4,192]{2,0,1,4,3:T(8,128)(2,1)} %bitcast.510) | data formatting | bytes 3440640 | tf_op jit(solution)/shard_map/all_to_all | solution.py:179
  317.2 83.1 %copy.341 = bf16[32,10,14,1536]{0,2,1,3:T(8,128)(2,1)} copy(bf16[32,10,14,1536]{3,0,2,1:T(8,128)(2,1)} %convolution_convert_fusion) | data formatting | bytes 27525120
  400.3 72.3 %reshape.336 = bf16[1536,4480]{1,0:T(8,128)(2,1)} reshape(bf16[1536,10,14,32]{3,2,1,0:T(8,128)(2,1)} %bitcast.507) | data formatting | bytes 27525120
  473.3 106.3 %reduce-scatter.7.cloned.1.call-done = bf16[384,4480]{1,0:T(8,128)(2,1)} async-done(((bf16[1536,4480]{1,0:T(8,128)(2,1)}), bf16[384,4480]{1,0:T(8,128)(2,1)}) %reduce-scatter.7.cloned.1.call-update) | async-done | bytes 3440656
  579.7 18.2 %reshape.337 = bf16[384,10,14,32]{3,2,1,0:T(8,128)(2,1)} reshape(bf16[384,4480]{1,0:T(8,128)(2,1)} %reduce-scatter.7.cloned.1.call-done) | data formatting | bytes 6881280
  597.9 18.6 %copy.342 = bf16[32,10,14,384]{3,0,2,1:T(8,128)(2,1)} copy(bf16[32,10,14,384]{0,2,1,3:T(8,128)(2,1)} %bitcast.509) | data formatting | bytes 6881280
  623.7 31.4 %all-reduce.11.cloned.1.call-done = f32[32,768]{1,0:T(8,128)} async-done(((f32[32,768]{1,0:T(8,128)}), f32[32,768]{1,0:T(8,128)}) %all-reduce.11.cloned.1.call-update) | async-done | bytes 98320 | tf_op jit(solution)/shard_map/psum | solution.py:189
  660.2 11.1 psum.285
  673.6 9.1 fusion.14
  682.7 88.9 %all-gather.3.cloned.1.call-done = bf16[32,10,14,1536]{3,0,2,1:T(8,128)(2,1)} async-done(((bf16[32,10,14,384]{3,0,2,1:T(8,128)(2,1)}), bf16[32,10,14,1536]{3,0,2,1:T(8,128)(2,1)}) %all-gather.3.cloned.1.call-update) | async-done | bytes 13762576 | tf_op jit(solution)/shard_map/all_gather | solution.py:218
  931.9 18.1 %all-gather.5.cloned.1.call-done = bf16[32,10,14,768]{3,0,2,1:T(8,128)(2,1)} async-done(((bf16[8,10,14,768]{3,0,2,1:T(8,128)(2,1)}), bf16[32,10,14,768]{3,0,2,1:T(8,128)(2,1)}) %all-gather.5.cloned.1.call-update) | async-done | bytes 6881296 | tf_op jit(solution)/shard_map/all_gather | solution.py:253
  958.1 128.1 %all-reduce.15.cloned.1.call-done = (f32[3,3,128,768]{2,3,0,1:T(8,128)}, f32[3,3,128,768]{2,3,0,1:T(8,128)}) async-done(((f32[3,3,128,768]{2,3,0,1:T(8,128)}, f32[3,3,128,768]{2,3,0,1:T(8,128)}), (f32[3,3,128,768]{2,3,0,1:T(8,128)}, f32[3,3,128,768]{2,3,0,1:T(8,128)})) %all-reduce.15.cloned.1.call-update) | async-done | bytes 7077904 | tf_op jit(solution)/shard_map/psum | solution.py:278
  1109.5 9.7 fusion.269
  1122.9 12.1 all-reduce.4
  1135.0 42.5 %all-reduce.2 = (f32[768]{0:T(1024)S(1)}, f32[768]{0:T(1024)S(1)}, f32[768]{0:T(1024)}, f32[768]{0:T(1024)}, f32[768]{0:T(1024)}, /*index=5*/f32[768]{0:T(1024)}...) all-reduce(f32[768]{0:T(1024)S(1)} %get-tuple-element.135, ...), channel_id=1, replica_groups=mesh['dp'=8,'chan'=4] {'dp'}, use_global_device_ids=true, to_apply=%region_24.25 | all-reduce | flops 11137 | bytes 89096 | tf_op jit(solution)/shard_map/psum | solution.py:277
  1177.6 10.7 convert_add_fusion
  1188.3 272.9 %all-reduce.13.cloned.1.call-done = (f32[384,768]{1,0:T(8,128)}, f32[3,3,128,768]{2,3,0,1:T(8,128)}, f32[3,3,128,768]{2,3,0,1:T(8,128)}, f32[192,1536]{1,0:T(8,1...) async-done(((f32[384,768]{1,0:T(8,128)}, f32[3,3,128,768]{2,3,0,1:T(8,128)}, f32[3,3,128,768]{2,3,0,1:T(8,128)}, f32[192,1536]{1,0:T(8,128)}, f32[384,768]{1,0:T(8,128)}, ...) | async-done | bytes 11796496 | tf_op jit(solution)/shard_map/psum | solution.py:264
  (366 shorter events, 299.4 us)
Async XLA Ops:
  7.2 647.9 %copy-start = (bf16[768,384]{1,0:T(8,128)(2,1)S(1)}, bf16[768,384]{1,0:T(8,128)(2,1)}, u32[]{:S(2)}) copy-start(bf16[768,384]{1,0:T(8,128)(2,1)} %param.36) | copy-start | bytes 1769476
  7.2 134.8 %reduce-scatter.5.cloned.1.call-start = ((), (), s32[]{:S(2)}) async-start(), calls=%async_computation.4 | async-start | bytes 17203200 | tf_op jit(solution)/shard_map/reduce_scatter | solution.py:165
  48.5 93.5 %copy-start.94 = (f32[768]{0:T(1024)S(1)}, f32[768]{0:T(1024)}, u32[]{:S(2)}) copy-start(f32[768]{0:T(1024)} %param.24) | copy-start | bytes 9220
  48.5 93.5 %copy-start.96 = (f32[768]{0:T(1024)S(1)}, f32[768]{0:T(1024)}, u32[]{:S(2)}) copy-start(f32[768]{0:T(1024)} %param.23) | copy-start | bytes 9220
  49.9 110.8 %copy-start.98 = (pred[8]{0:T(512)(128)(4,1)}, pred[8]{0:T(512)(128)(4,1)S(1)}, u32[]{:S(2)}) copy-start(pred[8]{0:T(512)(128)(4,1)S(1)} %dynamic-slice_compare_fusion) | copy-start | bytes 28
  49.9 95.5 %copy-start.25 = (bf16[3,3,128,768]{2,3,1,0:T(8,128)(2,1)S(1)}, bf16[3,3,128,768]{2,3,1,0:T(8,128)(2,1)}, u32[]{:S(2)}) copy-start(bf16[3,3,128,768]{2,3,1,0:T(8,128)(2,1)} %copy.279) | copy-start | bytes 5308420
  219.8 26.1 %all-to-all-start = ((bf16[4,2,107520]{2,1,0:T(2,128)(2,1)}), bf16[4,2,107520]{2,1,0:T(2,128)(2,1)}, u32[]{:S(2)}, u32[]{:S(2)}) async-start(bf16[4,2,107520]{2,1,0:T(2,128)(2,1)} %reshape.338), calls=%async_computation.1 | async-start | bytes 3440640 | tf_op jit(solution)/shard_map/all_to_all | solution.py:179
  224.2 355.5 %reduce-scatter.7.cloned.1.call-start = ((), (), s32[]{:S(2)}) async-start(), calls=%async_computation.8 | async-start | bytes 17203200
  224.8 546.8 %copy-start.66 = (f32[1536]{0:T(1024)}, f32[1536]{0:T(1024)S(1)}, u32[]{:S(2)}) copy-start(f32[1536]{0:T(1024)S(1)} %get-tuple-element.165) | copy-start | bytes 18436
  224.8 546.8 %copy-start.68 = (f32[1536]{0:T(1024)}, f32[1536]{0:T(1024)S(1)}, u32[]{:S(2)}) copy-start(f32[1536]{0:T(1024)S(1)} %get-tuple-element.164) | copy-start | bytes 18436
  288.4 20.3 %copy-start.22 = (bf16[192,1536]{1,0:T(8,128)(2,1)S(1)}, bf16[192,1536]{1,0:T(8,128)(2,1)}, u32[]{:S(2)}) copy-start(bf16[192,1536]{1,0:T(8,128)(2,1)} %param.31) | copy-start | bytes 1769476
  472.6 182.4 %all-reduce.11.cloned.1.call-start = ((), (), s32[]{:S(2)}) async-start(), calls=%async_computation.5 | async-start | bytes 196608 | tf_op jit(solution)/shard_map/psum | solution.py:189
  623.6 148.0 %all-gather.3.cloned.1.call-start = ((), (), s32[]{:S(2)}) async-start(), calls=%async_computation.6 | async-start | bytes 17203200 | tf_op jit(solution)/shard_map/all_gather | solution.py:218
  783.1 35.9 %all-to-all-start.1 = ((bf16[32,10,14,192]{3,2,1,0:T(8,128)(2,1)}), bf16[32,10,14,192]{3,2,1,0:T(8,128)(2,1)}, u32[]{:S(2)}, u32[]{:S(2)}) async-start(bf16[32,10,14,192]{3,2,1,0:T(8,128)(2,1)} %copy.284), calls=%async_computation.2 | async-start | bytes 5242880 | tf_op jit(solution)/shard_map/all_to_all | solution.py:229
  787.7 162.4 %all-gather.5.cloned.1.call-start = ((), (), s32[]{:S(2)}) async-start(), calls=%async_computation.7 | async-start | bytes 8601600 | tf_op jit(solution)/shard_map/all_gather | solution.py:253
  900.2 186.0 %all-reduce.15.cloned.1.call-start = ((), (), s32[]{:S(2)}) async-start(), calls=%async_computation.10 | async-start | bytes 14155776 | tf_op jit(solution)/shard_map/psum | solution.py:278
  921.2 28.9 %copy-start.26 = (bf16[384,768]{1,0:T(8,128)(2,1)S(1)}, bf16[384,768]{1,0:T(8,128)(2,1)}, u32[]{:S(2)}) copy-start(bf16[384,768]{1,0:T(8,128)(2,1)} %param.22) | copy-start | bytes 1769476
  921.2 28.9 %copy-start.77 = (f32[768]{0:T(1024)S(1)}, f32[768]{0:T(1024)}, u32[]{:S(2)}) copy-start(f32[768]{0:T(1024)} %copy-done.76) | copy-start | bytes 9220
  921.2 540.0 %all-reduce.13.cloned.1.call-start = ((), (), s32[]{:S(2)}) async-start(), calls=%async_computation.9 | async-start | bytes 23592960 | tf_op jit(solution)/shard_map/psum | solution.py:264
  1119.3 15.7 %copy-start.93 = (f32[384]{0:T(512)S(1)}, f32[384]{0:T(512)}, u32[]{:S(2)}) copy-start(f32[384]{0:T(512)} %get-tuple-element.99) | copy-start | bytes 4612
  1119.3 15.7 %copy-start.101 = (f32[384]{0:T(512)S(1)}, f32[384]{0:T(512)}, u32[]{:S(2)}) copy-start(f32[384]{0:T(512)} %get-tuple-element.161) | copy-start | bytes 4612
  1119.3 58.3 %copy-start.75 = (f32[768]{0:T(1024)S(1)}, f32[768]{0:T(1024)}, u32[]{:S(2)}) copy-start(f32[768]{0:T(1024)} %copy-done.74) | copy-start | bytes 9220
  1177.6 283.6 %copy-start.65 = (f32[768]{0:T(1024)S(1)}, f32[768]{0:T(1024)}, u32[]{:S(2)}) copy-start(f32[768]{0:T(1024)} %copy-done.64) | copy-start | bytes 9220
  1177.6 287.0 %copy-start.81 = (f32[768]{0:T(1024)S(1)}, f32[768]{0:T(1024)}, u32[]{:S(2)}) copy-start(f32[768]{0:T(1024)} %copy-done.80) | copy-start | bytes 9220
  (95 other events, 323.1 us)
Sparse Core Ops, SparseCore 0:
  34.7 107.1 reduce-scatter.4
  472.8 106.8 reduce-scatter.6
  623.7 31.2 all-reduce.10
  682.8 88.7 all-gather.2
  900.3 49.7 all-gather.4
  953.6 132.5 all-reduce.14
  1093.7 367.4 all-reduce.12
